TPU v7x, 128 devices: a whole 4x4x4 slice. The times are simulated.
128 devices in a mesh: fsdp: 4 (over x_hi, core), ctx: 32 (over y, z, x_lo).
Axes of the slice: x: 4 (x_hi: 2, x_lo: 2; x = x_hi * 2 + x_lo), y: 4, z: 4, core: 2. Of those that a mesh axis runs over, the one named last changes fastest.
Arguments:
- query_branch: bfloat16 [4, 8192, 4096], P('fsdp', 'ctx'), may hold values from -6 to 6
- key_branch: bfloat16 [4, 8192, 4096], P('fsdp', 'ctx'), may hold values from -6 to 6
- value_branch: bfloat16 [4, 8192, 4096], P('fsdp', 'ctx'), may hold values from -6 to 6
- cotangent: bfloat16 [4, 8192, 4096], P('fsdp', 'ctx'), may hold values from -6 to 6
- quantized_weight_codes: int32 [4096, 4096], P('ctx', 'fsdp'), may hold values from 0 to 15
- scale_code_bytes: int32 [4096, 64], P('ctx', 'fsdp'), may hold values from 0 to 255
- row_scale_second: float32 [4096], P('ctx'), may hold values from 0.01 to 0.1
- filters: bfloat16 [256, 128], replicated, may hold values from -0.5 to 0.5
- channel_skip_weight: float32 [4096], replicated, may hold values from -6 to 6
- adapter_down_weight: bfloat16 [4096, 64], P('ctx'), may hold values from -0.09375 to 0.09375
- adapter_up_weight: bfloat16 [64, 4096], P(None, 'fsdp'), may hold values from -0.75 to 0.75
Outputs:
- output: bfloat16 [4, 8192, 4096], P('fsdp', 'ctx')
- grad_query: bfloat16 [4, 8192, 4096], P('fsdp', 'ctx')
- grad_key: bfloat16 [4, 8192, 4096], P('fsdp', 'ctx')
- grad_value: bfloat16 [4, 8192, 4096], P('fsdp', 'ctx')
- grad_down: bfloat16 [4096, 64], P('ctx')
- grad_up: bfloat16 [64, 4096], P(None, 'fsdp')
All inputs are finite; a program needn't handle non-finite values.
Results may differ from a plain program's by a relative error of at most 0.0067.
Values may be sent and summed in bfloat16 or wider, within the bound.
No kernel may reach another device: no remote copies, remote signals or barrier semaphores. Data moves between devices by JAX's collectives and lax.ppermute only.
A program may use at most 256 MiB of HBM per device.

v0:
```python
import math
import jax
import jax.numpy as jnp
from jax import lax
from jax.sharding import PartitionSpec as P

QBLOCK = 64
normal_levels = (
    -1.0,
    -0.6961928009986877,
    -0.5250730514526367,
    -0.39491748809814453,
    -0.28444138169288635,
    -0.18477343022823334,
    -0.09105003625154495,
    0.0,
    0.07958029955625534,
    0.16093020141124725,
    0.24611230194568634,
    0.33791524171829224,
    0.44070982933044434,
    0.5626170039176941,
    0.7229568362236023,
    1.0,
)
adapter_scale = 0.25


def from_behind(shard, axis, by):
    count = lax.axis_size(axis)
    pairs = [(i, i + by) for i in range(count) if 0 <= i + by < count]
    return lax.ppermute(shard, axis, pairs)


def dequantize(quantized_weight_codes, scale_code_bytes, row_scale_second):
    levels = jnp.zeros(quantized_weight_codes.shape, jnp.float32)
    for number in range(16):
        levels = jnp.where(quantized_weight_codes == number, normal_levels[number], levels)
    absmax = row_scale_second[:, None] * (scale_code_bytes.astype(jnp.float32) + 1.0) / 256.0
    absmax = jnp.repeat(absmax, QBLOCK, axis=1)
    return (levels * absmax).astype(jnp.bfloat16)


def toeplitz(filter_taps, filter_len):
    groups = filter_taps.shape[0]
    padded = jnp.concatenate([filter_taps, jnp.zeros((groups, filter_len), filter_taps.dtype)], 1)
    repeated = jnp.tile(padded, (1, filter_len))[:, : filter_len * (2 * filter_len - 1)]
    return repeated.reshape(groups, filter_len, 2 * filter_len - 1)


def block_conv(extended, toep, filter_len):
    row_count = extended.shape[0] - (filter_len - 1)
    blocks = row_count // filter_len
    current = extended[:row_count].reshape(blocks, filter_len, -1)
    following = jnp.concatenate(
        [extended[filter_len:], jnp.zeros((1, extended.shape[1]), extended.dtype)], 0
    )
    following = following.reshape(blocks, filter_len, -1)[:, : filter_len - 1]
    windows = jnp.concatenate([current, following], 1)
    windows = windows.reshape(blocks, 2 * filter_len - 1, toep.shape[0], -1)
    result = jnp.einsum("gts,bsgk->btgk", toep, windows, preferred_element_type=jnp.float32)
    return result.reshape(row_count, -1)


def local(
    query_branch,
    key_branch,
    value_branch,
    cotangent,
    quantized_weight_codes,
    scale_code_bytes,
    row_scale_second,
    filters,
    channel_skip_weight,
    adapter_down_weight,
    adapter_up_weight,
):
    filter_len = filters.shape[1]
    queries = query_branch[0]
    output_gradient = cotangent[0]
    row_count, channels = queries.shape
    token_count = query_branch.shape[0] * row_count * lax.axis_size("ctx") * lax.axis_size("fsdp")
    multiplier = adapter_scale / math.sqrt(token_count)
    query_float = queries.astype(jnp.float32)
    key_float = key_branch[0].astype(jnp.float32)
    value_float = value_branch[0].astype(jnp.float32)
    mixed = (key_float * value_float).astype(jnp.bfloat16)
    before = from_behind(mixed[row_count - (filter_len - 1) :], "ctx", 1)
    ahead_toep = toeplitz(jnp.flip(filters, 1), filter_len)
    back_toep = toeplitz(filters, filter_len)
    gated = block_conv(
        jnp.concatenate([before, mixed], 0), ahead_toep, filter_len
    ) + channel_skip_weight * mixed.astype(jnp.float32)
    gated_signal = (query_float * gated).astype(jnp.bfloat16)
    local_piece = dequantize(quantized_weight_codes, scale_code_bytes, row_scale_second)
    local_rows, up_complete = (
        lax.all_gather(local_piece, "fsdp", axis=1, tiled=True),
        lax.all_gather(adapter_up_weight, "fsdp", axis=1, tiled=True),
    )
    backward_up_term = jnp.einsum(
        "td,rd->tr", output_gradient, up_complete, preferred_element_type=jnp.float32
    ).astype(jnp.bfloat16)
    weight_rows = lax.all_gather(local_rows, "ctx", axis=0, tiled=True)
    rank_rows = lax.all_gather(adapter_down_weight, "ctx", axis=0, tiled=True)
    output_total = jnp.dot(gated_signal, weight_rows, preferred_element_type=jnp.float32)
    down_sum = jnp.dot(gated_signal, rank_rows, preferred_element_type=jnp.float32)
    elementwise_product = jnp.einsum(
        "td,cd->tc", output_gradient, weight_rows, preferred_element_type=jnp.float32
    )
    elementwise_product = elementwise_product + adapter_scale * jnp.einsum(
        "tr,cr->tc", backward_up_term, rank_rows, preferred_element_type=jnp.float32
    )
    down_projection = down_sum.astype(jnp.bfloat16)
    output = (
        output_total
        + adapter_scale * jnp.dot(down_projection, up_complete, preferred_element_type=jnp.float32)
    ).astype(jnp.bfloat16)
    grad_query = (elementwise_product * gated).astype(jnp.bfloat16)
    grad_gated = (elementwise_product * query_float).astype(jnp.bfloat16)
    leading = jnp.concatenate(
        [jnp.zeros((filter_len, channels), jnp.bfloat16), grad_gated[: filter_len - 1]], 0
    )
    spill = block_conv(leading, back_toep, filter_len)
    arrived = from_behind(spill[1:], "ctx", -1)
    tail_rows = jnp.concatenate(
        [grad_gated, jnp.zeros((filter_len - 1, channels), jnp.bfloat16)], 0
    )
    local_grad = block_conv(tail_rows, back_toep, filter_len)
    local_grad = local_grad + jnp.concatenate(
        [jnp.zeros((row_count - filter_len + 1, channels), jnp.float32), arrived], 0
    )
    grad_mixed = local_grad + channel_skip_weight * grad_gated.astype(jnp.float32)
    grad_key = (grad_mixed * value_float).astype(jnp.bfloat16)
    grad_value = (grad_mixed * key_float).astype(jnp.bfloat16)
    term_down = multiplier * jnp.einsum(
        "tc,tr->cr", gated_signal, backward_up_term, preferred_element_type=jnp.float32
    )
    term_up = multiplier * jnp.einsum(
        "tr,td->rd", down_projection, output_gradient, preferred_element_type=jnp.float32
    )
    total_down = lax.psum(term_down, "fsdp")
    grad_down = lax.psum_scatter(total_down, "ctx", scatter_dimension=0, tiled=True)
    total_up = lax.psum(term_up, "ctx")
    grad_up = lax.psum_scatter(total_up, "fsdp", scatter_dimension=1, tiled=True)
    return (
        output[None],
        grad_query[None],
        grad_key[None],
        grad_value[None],
        grad_down.astype(jnp.bfloat16),
        grad_up.astype(jnp.bfloat16),
    )


def solution(mesh):
    return jax.shard_map(
        local,
        mesh=mesh,
        in_specs=(
            P("fsdp", "ctx", None),
            P("fsdp", "ctx", None),
            P("fsdp", "ctx", None),
            P("fsdp", "ctx", None),
            P("ctx", "fsdp"),
            P("ctx", "fsdp"),
            P("ctx"),
            P(),
            P(),
            P("ctx", None),
            P(None, "fsdp"),
        ),
        out_specs=(
            P("fsdp", "ctx", None),
            P("fsdp", "ctx", None),
            P("fsdp", "ctx", None),
            P("fsdp", "ctx", None),
            P("ctx", None),
            P(None, "fsdp"),
        ),
        check_vma=False,
    )
```

profile of v0, /device:TPU:1, one launch (start us, length us, event | category | flops | bytes accessed | tf_op | source)
XLA Modules:
  0.0 1086.2 jit_solution(9586040226539737358)
XLA Ops:
  10.7 24.5 %all-gather.3.cloned.1.call-done = bf16[128,4096]{0,1:T(8,128)(2,1)} async-done(((bf16[128,1024]{0,1:T(8,128)(2,1)}), bf16[128,4096]{0,1:T(8,128)(2,1)}) %all-gather.3.cloned.1.call-update) | async-done | bytes 1048592 | tf_op jit(solution)/shard_map/all_gather | solution.py:97
  46.3 41.7 %copy.62 = bf16[32,8,128,256]{3,1,2,0:T(8,128)(2,1)S(1)} copy(bf16[32,8,128,256]{3,2,1,0:T(8,128)(2,1)S(1)} %bitcast.101) | data formatting | bytes 33554432
  88.0 6.6 slice.54
  94.6 56.8 %reshape.84 = bf16[256,128,255,1]{2,1,0,3:T(8,128)(2,1)} reshape(bf16[256,32640]{1,0:T(8,128)(2,1)} %slice.54) | data formatting | bytes 33423360 | tf_op jit(solution)/shard_map/reshape | solution.py:48
  151.3 56.7 %reshape.76 = bf16[256,128,255]{2,1,0:T(8,128)(2,1)} reshape(bf16[256,32640]{1,0:T(8,128)(2,1)} %slice.54) | data formatting | bytes 33423360 | tf_op jit(solution)/shard_map/reshape | solution.py:48
  209.3 41.7 %copy.60 = bf16[32,8,128,256]{3,1,2,0:T(8,128)(2,1)S(1)} copy(bf16[32,8,128,256]{3,2,1,0:T(8,128)(2,1)S(1)} %bitcast.102) | data formatting | bytes 33554432
  251.0 6.6 slice.52
  257.6 56.8 %reshape.83 = bf16[256,128,255,1]{2,1,0,3:T(8,128)(2,1)} reshape(bf16[256,32640]{1,0:T(8,128)(2,1)} %slice.52) | data formatting | bytes 33423360 | tf_op jit(solution)/shard_map/reshape | solution.py:48
  317.6 4.2 copy.57
  321.8 12.4 %all_gather.15 = bf16[64,4096]{1,0:T(8,128)(2,1)S(1)} all-gather(bf16[64,1024]{1,0:T(8,128)(2,1)S(1)} %copy-done.11), channel_id=1, replica_groups=mesh['fsdp'=4,'ctx'=32] {'fsdp'}, dimensions={1}, use_global_device_ids=true | all-gather | bytes 655360 | tf_op jit(solution)/shard_map/all_gather | solution.py:98
  334.1 80.4 %all_gather.14 = bf16[4096,64]{0,1:T(8,128)(2,1)S(1)} all-gather(bf16[128,64]{0,1:T(8,128)(2,1)S(1)} %copy-done.13), channel_id=1, replica_groups=mesh['fsdp'=4,'ctx'=32] {'ctx'}, dimensions={0}, use_global_device_ids=true | all-gather | bytes 540672 | tf_op jit(solution)/shard_map/all_gather | solution.py:104
  418.2 4.1 copy.23
  422.3 4.0 concatenate.44
  426.3 3.4 copy.25
  429.7 9.5 fusion.19
  443.6 5.7 copy.28
  449.2 329.5 %all-gather.5.cloned.1.call-done = bf16[4096,4096]{0,1:T(8,128)(2,1)} async-done(((bf16[128,4096]{0,1:T(8,128)(2,1)}), bf16[4096,4096]{0,1:T(8,128)(2,1)}) %all-gather.5.cloned.1.call-update) | async-done | bytes 33554448 | tf_op jit(solution)/shard_map/all_gather | solution.py:103
  778.8 17.2 %convolution_bitcast_fusion = f32[256,4096]{1,0:T(8,128)} fusion(bf16[4096,4096]{0,1:T(8,128)(2,1)} %all-gather.5.cloned.1.call-done, bf16[1,256,4096]{2,1,0:T(8,128)(2,1)S(1)} %copy-done), kind=kOutput, calls=%fused_computation.4 | convolution fusion | flops 8589934592 | bytes 39845888 | tf_op jit(solution)/shard_map/td,cd->tc/dot_general | solution.py:107
  796.0 6.7 fusion.29
  814.0 12.6 %convolution_bitcast_fusion.1 = f32[1,128,256,16]{1,3,2,0:T(8,128)} fusion(bf16[255,256,16]{0,2,1:T(8,128)(2,1)} %bitcast.111, bf16[256,128,255]{2,1,0:T(8,128)(2,1)} %reshape.76), kind=kOutput, calls=%fused_computation.45 | convolution fusion | flops 267386880 | bytes 20897792 | tf_op jit(solution)/shard_map/gts,bsgk->btgk/dot_general | solution.py:61
  826.6 3.7 slice.57
  837.6 17.7 %fusion.43 = f32[256,4096]{1,0:T(8,128)} fusion(bf16[256,4096]{1,0:T(8,128)(2,1)} %copy-done.6, bf16[4096,4096]{0,1:T(8,128)(2,1)} %all-gather.5.cloned.1.call-done), kind=kOutput, calls=%fused_computation.55 | convolution fusion | flops 8589934592 | bytes 39845888 | tf_op jit(solution)/shard_map/dot_general | solution.py:105
  855.3 4.1 copy.46
  859.4 4.0 concatenate.49
  863.3 3.3 copy.48
  868.3 4.2 copy.58
  872.5 9.9 fusion.24
  886.9 5.7 copy.53
  892.5 4.4 fusion.7
  896.9 6.5 fusion.30
  903.4 135.5 %all-reduce.8 = bf16[64,1024]{1,0:T(8,128)(2,1)} all-reduce(f32[64,1024]{1,0:T(8,128)} %reduce-scatter.5.cloned.1.call-done), channel_id=1, replica_groups=mesh['fsdp'=4,'ctx'=32] {'ctx'}, use_global_device_ids=true, to_apply=%region_2.3 | all-reduce | flops 65536 | bytes 393216 | tf_op jit(solution)/shard_map/psum | solution.py:143
  1038.9 40.4 %psum.16 = bf16[128,64]{0,1:T(8,128)(2,1)} all-reduce(f32[128,64]{0,1:T(8,128)} %reduce-scatter.3.cloned.1.call-done), channel_id=1, replica_groups=mesh['fsdp'=4,'ctx'=32] {'fsdp'}, use_global_device_ids=true, to_apply=%region_0.1 | all-reduce | flops 8192 | bytes 49152 | tf_op jit(solution)/shard_map/psum | solution.py:141
  (71 shorter events, 51.8 us)
Async XLA Ops:
  7.2 407.4 %copy-start = (bf16[1,256,4096]{2,1,0:T(8,128)(2,1)S(1)}, bf16[1,256,4096]{2,1,0:T(8,128)(2,1)}, u32[]{:S(2)}) copy-start(bf16[1,256,4096]{2,1,0:T(8,128)(2,1)} %param.14) | copy-start | bytes 6291460
  7.2 28.0 %all-gather.3.cloned.1.call-start = ((), (), s32[]{:S(2)}) async-start(), calls=%async_computation.2 | async-start | bytes 1310720 | tf_op jit(solution)/shard_map/all_gather | solution.py:97
  10.6 768.1 %all-gather.5.cloned.1.call-start = ((), (), s32[]{:S(2)}) async-start(), calls=%async_computation.3 | async-start | bytes 34603008 | tf_op jit(solution)/shard_map/all_gather | solution.py:103
  35.2 868.2 %reduce-scatter.5.cloned.1.call-start = ((), (), s32[]{:S(2)}) async-start(), calls=%async_computation.5 | async-start | bytes 1310720 | tf_op jit(solution)/shard_map/reduce_scatter | solution.py:144
  38.2 4.7 copy-start.3
  38.2 6.5 copy-start.10
  39.8 375.6 %collective-permute-start = (bf16[127,4096]{1,0:T(8,128)(2,1)}, bf16[127,4096]{1,0:T(8,128)(2,1)}, u32[]{:S(2)}, u32[]{:S(2)}) collective-permute-start(bf16[127,4096]{1,0:T(8,128)(2,1)} %slice.49), channel_id=1, source_target_pairs={{0,1},{1,2},{2,3},{3,4},{4,5},{5,6},{6,7},{7,8},{8,9},{9,10},{10,1... | collective-permute-start | bytes 3121160 | tf_op jit(solution)/shard_map/ppermute | solution.py:32
  314.4 7.4 copy-start.11
  314.4 19.7 %copy-start.13 = (bf16[128,64]{0,1:T(8,128)(2,1)S(1)}, bf16[128,64]{0,1:T(8,128)(2,1)}, u32[]{:S(2)}) copy-start(bf16[128,64]{0,1:T(8,128)(2,1)} %param.20) | copy-start | bytes 49156
  321.8 93.6 %copy-start.4 = (bf16[256,4096]{1,0:T(8,128)(2,1)S(1)}, bf16[256,4096]{1,0:T(8,128)(2,1)}, u32[]{:S(2)}) copy-start(bf16[256,4096]{1,0:T(8,128)(2,1)} %copy-done.3) | copy-start | bytes 6291460
  426.3 3.4 copy-start.7
  449.2 346.7 %copy-start.12 = (f32[4096]{0:T(1024)S(1)}, f32[4096]{0:T(1024)}, u32[]{:S(2)}) copy-start(f32[4096]{0:T(1024)} %param.19) | copy-start | bytes 49156
  778.8 17.2 %copy-start.5 = (bf16[256,4096]{1,0:T(8,128)(2,1)S(1)}, bf16[256,4096]{1,0:T(8,128)(2,1)}, u32[]{:S(2)}) copy-start(bf16[256,4096]{1,0:T(8,128)(2,1)} %copy-done.3) | copy-start | bytes 6291460
  778.8 17.2 %copy-start.9 = (f32[256,4096]{1,0:T(8,128)S(1)}, f32[256,4096]{1,0:T(8,128)}, u32[]{:S(2)}) copy-start(f32[256,4096]{1,0:T(8,128)} %copy.28) | copy-start | bytes 12582916
  802.7 1.3 copy-start.6
  802.7 3.8 copy-start.14
  806.2 232.7 %reduce-scatter.3.cloned.1.call-start = ((), (), s32[]{:S(2)}) async-start(), calls=%async_computation.4 | async-start | bytes 1081344 | tf_op jit(solution)/shard_map/reduce_scatter | solution.py:142
  833.2 63.7 %collective-permute-start.1 = (f32[127,4096]{1,0:T(8,128)}, f32[127,4096]{1,0:T(8,128)}, u32[]{:S(2)}, u32[]{:S(2)}) collective-permute-start(f32[127,4096]{1,0:T(8,128)} %copy.52), channel_id=1, source_target_pairs={{1,0},{2,1},{3,2},{4,3},{5,4},{6,5},{7,6},{8,7},{9,8},{10,9},{11,1... | collective-permute-start | bytes 6242312 | tf_op jit(solution)/shard_map/ppermute | solution.py:32
  863.3 3.3 copy-start.1
  892.5 4.4 copy-start.2
  892.5 4.4 copy-start.8
Sparse Core Ops, SparseCore 0:
  10.8 24.3 all-gather.2
  36.7 742.0 all-gather.4
  806.4 30.7 reduce-scatter.4
  839.4 139.4 reduce-scatter.2
where the time goes:
time: 1100 us; the launch traced here: 1090 us
  waiting for transfers between devices  354 us (32%)
  local copies, waits for them, and re-layouts  344 us (31%)
  blocking collectives  269 us (24%)
  matrix products  84 us (8%)
  other arithmetic  16.8 us (2%)
  between operations  14.3 us (1%)
    all_gather x1, waiting for transfers between devices, local(): weight_rows = lax.all_gather(local_rows, 'ctx', axis=0, tiled=True)  330 us
    reshape x3, local copies, waits for them, and re-layouts, toeplitz(): return repeated.reshape(groups, filter_len, 2 * filter_len - 1)  170 us
    psum x1, blocking collectives, local(): total_up = lax.psum(term_up, 'ctx')  135 us
    unnamed x38, local copies, waits for them, and re-layouts  101 us
    all_gather x1, blocking collectives, local(): rank_rows = lax.all_gather(adapter_down_weight, 'ctx', axis=0, tiled=True)  80.4 us
    psum x1, blocking collectives, local(): total_down = lax.psum(term_down, 'fsdp')  40.4 us
    dot_general x3, matrix products, block_conv(): jnp.einsum('gts,bsgk->btgk', toep, windows, preferred_element_type=jnp.fl...  32 us
    all_gather x1, waiting for transfers between devices, local(): lax.all_gather(local_piece, 'fsdp', axis=1, tiled=True)  24.5 us
  transfers between devices with their start and end apart: 6, of which 2 were waited for; matrix products, arithmetic and copies ran while one was open for 38% of the time, Pallas kernels for 0%

commit v1 on v0

--- a/solution.py
+++ b/solution.py
@@ -138,7 +138,7 @@
     term_up = multiplier * jnp.einsum(
         "tr,td->rd", down_projection, output_gradient, preferred_element_type=jnp.float32
     )
-    total_down = lax.psum(term_down, "fsdp")
+    total_down = jnp.sum(lax.all_gather(term_down, "fsdp"), axis=0)
     grad_down = lax.psum_scatter(total_down, "ctx", scatter_dimension=0, tiled=True)
     total_up = lax.psum(term_up, "ctx")
     grad_up = lax.psum_scatter(total_up, "fsdp", scatter_dimension=1, tiled=True)

time: 1100 us -> 1250 us (1.14)
  the two profiles are of different devices: /device:TPU:1 before, /device:TPU:0 now
where the time goes in v1:
time: 1250 us
  waiting for transfers between devices  505 us (40%)
  local copies, waits for them, and re-layouts  350 us (28%)
  blocking collectives  265 us (21%)
  matrix products  84.2 us (7%)
  other arithmetic  24 us (2%)
  between operations  14.3 us (1%)
    all_gather x1, waiting for transfers between devices, local(): weight_rows = lax.all_gather(local_rows, 'ctx', axis=0, tiled=True)  482 us
    reshape x3, local copies, waits for them, and re-layouts, toeplitz(): return repeated.reshape(groups, filter_len, 2 * filter_len - 1)  170 us
    psum x1, blocking collectives, local(): total_up = lax.psum(term_up, 'ctx')  162 us
    unnamed x42, local copies, waits for them, and re-layouts  101 us
    all_gather x1, blocking collectives, local(): rank_rows = lax.all_gather(adapter_down_weight, 'ctx', axis=0, tiled=True)  91.4 us
    dot_general x3, matrix products, block_conv(): jnp.einsum('gts,bsgk->btgk', toep, windows, preferred_element_type=jnp.fl...  31.6 us
  transfers between devices with their start and end apart: 7, of which 2 were waited for; matrix products, arithmetic and copies ran while one was open for 34% of the time, Pallas kernels for 0%

profile of v1, /device:TPU:0, one launch (start us, length us, event | category | flops | bytes accessed | tf_op | source)
XLA Modules:
  0.0 1247.9 jit_solution(10605540162486815227)
XLA Ops:
  10.7 23.3 %all-gather.5.cloned.1.call-done = bf16[128,4096]{0,1:T(8,128)(2,1)} async-done(((bf16[128,1024]{0,1:T(8,128)(2,1)}), bf16[128,4096]{0,1:T(8,128)(2,1)}) %all-gather.5.cloned.1.call-update) | async-done | bytes 1048592 | tf_op jit(solution)/shard_map/all_gather | solution.py:97
  38.6 3.4 collective-permute-start
  45.4 41.7 %copy.60 = bf16[32,8,128,256]{3,1,2,0:T(8,128)(2,1)S(1)} copy(bf16[32,8,128,256]{3,2,1,0:T(8,128)(2,1)S(1)} %bitcast.103) | data formatting | bytes 33554432
  87.1 6.6 slice.52
  93.7 56.8 %reshape.84 = bf16[256,128,255,1]{2,1,0,3:T(8,128)(2,1)} reshape(bf16[256,32640]{1,0:T(8,128)(2,1)} %slice.52) | data formatting | bytes 33423360 | tf_op jit(solution)/shard_map/reshape | solution.py:48
  153.6 4.1 copy.57
  157.8 12.0 all_gather.21
  169.7 91.4 %all_gather.20 = bf16[4096,64]{0,1:T(8,128)(2,1)S(1)} all-gather(bf16[128,64]{0,1:T(8,128)(2,1)S(1)} %copy-done.15), channel_id=1, replica_groups=mesh['fsdp'=4,'ctx'=32] {'ctx'}, dimensions={0}, use_global_device_ids=true | all-gather | bytes 540672 | tf_op jit(solution)/shard_map/all_gather | solution.py:104
  264.8 4.1 copy.23
  268.9 4.0 concatenate.44
  276.2 9.5 fusion.19
  290.2 5.7 copy.28
  295.8 482.0 %all-gather.7.cloned.1.call-done = bf16[4096,4096]{0,1:T(8,128)(2,1)} async-done(((bf16[128,4096]{0,1:T(8,128)(2,1)}), bf16[4096,4096]{0,1:T(8,128)(2,1)}) %all-gather.7.cloned.1.call-update) | async-done | bytes 33554448 | tf_op jit(solution)/shard_map/all_gather | solution.py:103
  777.8 17.2 %convolution_bitcast_fusion = f32[256,4096]{1,0:T(8,128)} fusion(bf16[4096,4096]{0,1:T(8,128)(2,1)} %all-gather.7.cloned.1.call-done, bf16[1,256,4096]{2,1,0:T(8,128)(2,1)S(1)} %copy-done), kind=kOutput, calls=%fused_computation.4 | convolution fusion | flops 8589934592 | bytes 39845888 | tf_op jit(solution)/shard_map/td,cd->tc/dot_general | solution.py:107
  795.0 6.7 fusion.29
  806.1 41.7 %copy.62 = bf16[32,8,128,256]{3,1,2,0:T(8,128)(2,1)S(1)} copy(bf16[32,8,128,256]{3,2,1,0:T(8,128)(2,1)S(1)} %bitcast.104) | data formatting | bytes 33554432
  847.8 6.5 slice.54
  854.3 56.7 %reshape.85 = bf16[256,128,255,1]{2,1,0,3:T(8,128)(2,1)} reshape(bf16[256,32640]{1,0:T(8,128)(2,1)} %slice.54) | data formatting | bytes 33423360 | tf_op jit(solution)/shard_map/reshape | solution.py:48
  911.1 56.7 %reshape.76 = bf16[256,128,255]{2,1,0:T(8,128)(2,1)} reshape(bf16[256,32640]{1,0:T(8,128)(2,1)} %slice.54) | data formatting | bytes 33423360 | tf_op jit(solution)/shard_map/reshape | solution.py:48
  975.3 12.2 convolution_bitcast_fusion.1
  987.5 3.5 slice.57
  999.4 18.3 %fusion.43 = f32[256,4096]{1,0:T(8,128)} fusion(bf16[256,4096]{1,0:T(8,128)(2,1)} %copy-done.6, bf16[4096,4096]{0,1:T(8,128)(2,1)} %all-gather.7.cloned.1.call-done), kind=kOutput, calls=%fused_computation.55 | convolution fusion | flops 8589934592 | bytes 39845888 | tf_op jit(solution)/shard_map/dot_general | solution.py:105
  1017.6 4.1 copy.46
  1021.7 4.0 concatenate.49
  1030.7 4.2 copy.58
  1034.9 6.1 reshape.83
  1041.0 5.8 reduce_sum.9
  1046.9 9.9 fusion.24
  1061.2 6.0 copy.53
  1067.2 4.4 fusion.7
  1071.6 6.5 fusion.30
  1078.1 161.7 %all-reduce.8 = bf16[64,1024]{1,0:T(8,128)(2,1)} all-reduce(f32[64,1024]{1,0:T(8,128)} %reduce-scatter.5.cloned.1.call-done), channel_id=1, replica_groups=mesh['fsdp'=4,'ctx'=32] {'ctx'}, use_global_device_ids=true, to_apply=%region_2.3 | all-reduce | flops 65536 | bytes 393216 | tf_op jit(solution)/shard_map/psum | solution.py:143
  (80 shorter events, 57.0 us)
Async XLA Ops:
  7.2 254.0 %copy-start = (bf16[1,256,4096]{2,1,0:T(8,128)(2,1)S(1)}, bf16[1,256,4096]{2,1,0:T(8,128)(2,1)}, u32[]{:S(2)}) copy-start(bf16[1,256,4096]{2,1,0:T(8,128)(2,1)} %param.14) | copy-start | bytes 6291460
  7.2 26.8 %all-gather.5.cloned.1.call-start = ((), (), s32[]{:S(2)}) async-start(), calls=%async_computation.2 | async-start | bytes 1310720 | tf_op jit(solution)/shard_map/all_gather | solution.py:97
  10.6 767.2 %all-gather.7.cloned.1.call-start = ((), (), s32[]{:S(2)}) async-start(), calls=%async_computation.3 | async-start | bytes 34603008 | tf_op jit(solution)/shard_map/all_gather | solution.py:103
  34.0 1000.9 %all-gather.9.cloned.1.call-start = ((), (), s32[]{:S(2)}) async-start(), calls=%async_computation.5 | async-start | bytes 5242880 | tf_op jit(solution)/shard_map/all_gather | solution.py:141
  37.1 5.0 copy-start.3
  37.1 6.8 copy-start.12
  38.6 223.3 %collective-permute-start = (bf16[127,4096]{1,0:T(8,128)(2,1)}, bf16[127,4096]{1,0:T(8,128)(2,1)}, u32[]{:S(2)}, u32[]{:S(2)}) collective-permute-start(bf16[127,4096]{1,0:T(8,128)(2,1)} %slice.49), channel_id=1, source_target_pairs={{0,1},{1,2},{2,3},{3,4},{4,5},{5,6},{6,7},{7,8},{8,9},{9,10},{10,1... | collective-permute-start | bytes 3121160 | tf_op jit(solution)/shard_map/ppermute | solution.py:32
  150.4 7.3 copy-start.13
  150.4 19.3 %copy-start.15 = (bf16[128,64]{0,1:T(8,128)(2,1)S(1)}, bf16[128,64]{0,1:T(8,128)(2,1)}, u32[]{:S(2)}) copy-start(bf16[128,64]{0,1:T(8,128)(2,1)} %param.20) | copy-start | bytes 49156
  157.7 104.2 %copy-start.4 = (bf16[256,4096]{1,0:T(8,128)(2,1)S(1)}, bf16[256,4096]{1,0:T(8,128)(2,1)}, u32[]{:S(2)}) copy-start(bf16[256,4096]{1,0:T(8,128)(2,1)} %copy-done.3) | copy-start | bytes 6291460
  169.7 91.4 %copy-start.10 = (bf16[64,4096]{1,0:T(8,128)(2,1)}, bf16[64,4096]{1,0:T(8,128)(2,1)S(1)}, u32[]{:S(2)}) copy-start(bf16[64,4096]{1,0:T(8,128)(2,1)S(1)} %all_gather.21) | copy-start | bytes 1572868
  272.9 3.3 copy-start.7
  295.8 499.2 %copy-start.14 = (f32[4096]{0:T(1024)S(1)}, f32[4096]{0:T(1024)}, u32[]{:S(2)}) copy-start(f32[4096]{0:T(1024)} %param.19) | copy-start | bytes 49156
  777.8 17.2 %copy-start.5 = (bf16[256,4096]{1,0:T(8,128)(2,1)S(1)}, bf16[256,4096]{1,0:T(8,128)(2,1)}, u32[]{:S(2)}) copy-start(bf16[256,4096]{1,0:T(8,128)(2,1)} %copy-done.3) | copy-start | bytes 6291460
  777.8 17.2 %copy-start.9 = (f32[256,4096]{1,0:T(8,128)S(1)}, f32[256,4096]{1,0:T(8,128)}, u32[]{:S(2)}) copy-start(f32[256,4096]{1,0:T(8,128)} %copy.28) | copy-start | bytes 12582916
  801.7 1.3 copy-start.6
  804.6 273.6 %reduce-scatter.5.cloned.1.call-start = ((), (), s32[]{:S(2)}) async-start(), calls=%async_computation.6 | async-start | bytes 1310720 | tf_op jit(solution)/shard_map/reduce_scatter | solution.py:144
  911.1 56.7 %copy-start.16 = (pred[128]{0:T(512)(128)(4,1)S(1)}, pred[128]{0:T(512)(128)(4,1)}, u32[]{:S(2)}) copy-start(pred[128]{0:T(512)(128)(4,1)} %constant.31.clone.1) | copy-start | bytes 388
  994.0 77.7 %collective-permute-start.1 = (f32[127,4096]{1,0:T(8,128)}, f32[127,4096]{1,0:T(8,128)}, u32[]{:S(2)}, u32[]{:S(2)}) collective-permute-start(f32[127,4096]{1,0:T(8,128)} %copy.52), channel_id=1, source_target_pairs={{1,0},{2,1},{3,2},{4,3},{5,4},{6,5},{7,6},{8,7},{9,8},{10,9},{11,1... | collective-permute-start | bytes 6242312 | tf_op jit(solution)/shard_map/ppermute | solution.py:32
  999.1 240.7 %reduce-scatter.3.cloned.1.call-start = ((), (), s32[]{:S(2)}) async-start(), calls=%async_computation.4 | async-start | bytes 1081344 | tf_op jit(solution)/shard_map/reduce_scatter | solution.py:142
  1025.7 3.3 copy-start.1
  1061.2 6.0 copy-start.11
  1067.2 4.4 copy-start.2
  1067.2 4.4 copy-start.8
Sparse Core Ops, SparseCore 0:
  10.8 23.1 all-gather.4
  35.6 742.1 all-gather.6
  804.7 37.6 all-gather.8
  999.2 33.1 reduce-scatter.4
  1047.0 163.6 reduce-scatter.2
